TPU v7x, 256 devices: a whole 4x4x8 slice. The times are simulated.
256 devices in a mesh: pair: 64 (over x_hi, z, y), sigma: 4 (over x_lo, core).
Axes of the slice: x: 4 (x_hi: 2, x_lo: 2; x = x_hi * 2 + x_lo), y: 4, z: 8, core: 2. Of those that a mesh axis runs over, the one named last changes fastest.
Arguments:
- pair_density_matrices: bfloat16 [131072, 1536], P('pair'), may hold values from -16 to 16
- energy_bins: int32 [131072, 2], P('pair'), may hold values from 0 to 63
- bin_weights: float32 [2, 64], replicated, may hold values from 0.05 to 1
- coulomb: float32 [1536], replicated, may hold values from 0.5 to 4
- state_matrices: bfloat16 [1536, 2048], P(None, 'sigma'), may hold values from -6 to 6
Outputs:
- screened_states: float32 [1536, 2, 2048], P('pair', None, 'sigma')
- sigma_diag: float32 [2, 2048], P(None, 'sigma')
All inputs are finite; a program needn't handle non-finite values.
Results may differ from a plain program's by a relative error of at most 0.00035.
Values sent between devices are 32-bit elements; how exact they have to be, the bound alone decides.
No kernel may reach another device: no remote copies, remote signals or barrier semaphores. Data moves between devices by JAX's collectives and lax.ppermute only.
A program may use at most 64 MiB of HBM per device.

v0:
```python
import jax
import jax.numpy as jnp
from jax import lax
from jax.sharding import PartitionSpec as P


def pair_weights(energy_bins, bin_weights, pair_total):
    bin_levels = jnp.arange(bin_weights.shape[1], dtype=jnp.int32)
    matches = (energy_bins[:, :, None] == bin_levels[None, None, :]).astype(jnp.float32)
    picked = jnp.sum(matches * bin_weights[None, :, :], axis=2)
    return picked.T / jnp.float32(pair_total)


def local(pair_density_matrices, energy_bins, bin_weights, coulomb, state_matrices):
    pair_local, width = pair_density_matrices.shape
    pair_count = lax.axis_size("pair")
    self_energy_count = lax.axis_size("sigma")
    row_count = width // pair_count
    col_count = width // self_energy_count
    pair_position = lax.axis_index("pair")
    sigma_pos = lax.axis_index("sigma")
    weight = pair_weights(energy_bins, bin_weights, pair_local * pair_count)
    column_slab = lax.dynamic_slice_in_dim(
        pair_density_matrices, sigma_pos * col_count, col_count, 1
    )
    scaled_product = (weight[:, :, None] * column_slab[None, :, :].astype(jnp.float32)).astype(
        jnp.bfloat16
    )
    polar_block = lax.psum_scatter(
        -jnp.einsum(
            "zh,vzo->hvo", pair_density_matrices, scaled_product, preferred_element_type=jnp.float32
        ),
        "pair",
        scatter_dimension=0,
        tiled=True,
    )
    coulomb_root = jnp.sqrt(coulomb)
    root_rows = lax.dynamic_slice_in_dim(coulomb_root, pair_position * row_count, row_count, 0)
    coulomb_root_columns = lax.dynamic_slice_in_dim(
        coulomb_root, sigma_pos * col_count, col_count, 0
    )
    screened = root_rows[:, None, None] * polar_block * coulomb_root_columns[None, None, :]
    states_wide = state_matrices.astype(jnp.float32)
    applied = jnp.einsum(
        "rfc,cn->rfn",
        lax.all_gather(screened, "sigma", axis=2, tiled=True),
        states_wide,
        precision=lax.Precision.HIGHEST,
    )
    own_states = lax.dynamic_slice_in_dim(states_wide, pair_position * row_count, row_count, 0)
    partial_contribution = jnp.sum(own_states[:, None, :] * applied, axis=0) / jnp.float32(width)
    sigma_diag = lax.psum(partial_contribution, "pair")
    return (applied, sigma_diag)


def solution(mesh):
    return jax.shard_map(
        local,
        mesh=mesh,
        in_specs=(P("pair", None), P("pair", None), P(), P(), P(None, "sigma")),
        out_specs=(P("pair", None, "sigma"), P(None, "sigma")),
        check_vma=False,
    )
```

profile of v0, /device:TPU:2, one launch (start us, length us, event | category | flops | bytes accessed | tf_op | source)
XLA Modules:
  0.0 1032.7 jit_solution(59104497414728657)
XLA Ops:
  7.2 0.0 reduce-scatter.2.cloned.1.call-start
  7.2 1.0 select_reduce_fusion
  8.2 1.6 dynamic-slice_convert_fusion
  9.9 10.4 %negate_bitcast_fusion = f32[1536,2,384]{2,0,1:T(8,128)} fusion(bf16[2048,1536]{1,0:T(8,128)(2,1)} %param.5, f32[2048,384]{1,0:T(8,128)S(1)} %dynamic-slice_convert_fusion, f32[2,2048]{1,0:T(2,128)S(1)} %multiply_bitcast_fusion), kind=kOutput, calls=%fused_computation.3 | convolution fusion | flops 4836163584 | bytes 14172160 | tf_op jit(solution)/shard_map/zh,vzo->hvo/dot_general | solution.py:30
  20.3 0.0 copy-start.1
  20.3 0.0 copy-start
  20.3 0.0 reduce-scatter.2.cloned.1.call-update
  20.3 0.7 copy-done.1
  21.0 0.1 dynamic_slice.14
  21.1 0.1 dynamic_slice.12
  21.2 0.6 copy-done
  21.7 814.2 %reduce-scatter.2.cloned.1.call-done = f32[24,2,384]{2,0,1:T(8,128)} async-done(((f32[1536,2,384]{2,0,1:T(8,128)}), f32[24,2,384]{2,0,1:T(8,128)}) %reduce-scatter.2.cloned.1.call-update) | async-done | bytes 73744 | tf_op jit(solution)/shard_map/reduce_scatter | solution.py:29
  836.0 1.0 multiply_multiply_fusion
  836.9 5.9 all_gather.3
  842.8 0.9 multiply_reduce_fusion
  843.7 0.7 copy.10
  844.4 181.4 %psum.7 = f32[2,512]{1,0:T(2,128)} all-reduce(f32[2,512]{1,0:T(2,128)S(1)} %broadcast_multiply_fusion), channel_id=1, replica_groups=mesh['pair'=64,'sigma'=4] {'pair'}, use_global_device_ids=true, to_apply=%region_3.0 | all-reduce | flops 1024 | bytes 8192 | tf_op jit(solution)/shard_map/psum | solution.py:52
  (4 shorter events, 0.0 us)
Async XLA Ops:
  7.2 828.8 %reduce-scatter.2.cloned.1.call-start = ((), (), s32[]{:S(2)}) async-start(), calls=%async_computation.1 | async-start | bytes 4792320 | tf_op jit(solution)/shard_map/reduce_scatter | solution.py:29
  20.3 0.7 copy-start.1
  20.3 1.4 copy-start
Sparse Core Ops, SparseCore 0:
  20.5 815.4 reduce-scatter.1
where the time goes:
time: 1030 us
  waiting for transfers between devices  814 us (79%)
  blocking collectives  187 us (18%)
  between operations  14.1 us (1%)
  matrix products  11.4 us (1%)
    reduce_scatter x1, waiting for transfers between devices, local(): lax.psum_scatter(-jnp.einsum('zh,vzo->hvo', pair_density_matrices, scaled...  814 us
    psum x1, blocking collectives, local(): sigma_diag = lax.psum(partial_contribution, 'pair')  181 us
  transfers between devices with their start and end apart: 1, of which 1 were waited for; matrix products, arithmetic and copies ran while one was open for 0% of the time, Pallas kernels for 0%

commit v1 on v0

--- a/solution.py
+++ b/solution.py
@@ -49,7 +49,7 @@
     )
     own_states = lax.dynamic_slice_in_dim(states_wide, pair_position * row_count, row_count, 0)
     partial_contribution = jnp.sum(own_states[:, None, :] * applied, axis=0) / jnp.float32(width)
-    sigma_diag = lax.psum(partial_contribution, "pair")
+    sigma_diag = jnp.sum(lax.all_gather(partial_contribution, "pair"), axis=0)
     return (applied, sigma_diag)
 
 

time: 1030 us -> 941 us (0.914)
  waiting for transfers between devices: 814 us -> 711 us
  local copies, waits for them, and re-layouts: 2.11 us -> 13.6 us
    reduce_scatter x1 -> x0, waiting for transfers between devices: 814 us -> none  [local(): lax.psum_scatter(-jnp.einsum('zh,vzo->hvo', pair_density_matrices, scaled...]
    unnamed x1 -> x2, waiting for transfers between devices: 0.02 us -> 711 us
    all_gather x0 -> x1, blocking collectives: none -> 181 us  [local(): sigma_diag = jnp.sum(lax.all_gather(partial_contribution, 'pair'), axis=0)]
    psum x1 -> x0, blocking collectives: 181 us -> none  [local(): sigma_diag = lax.psum(partial_contribution, 'pair')]
where the time goes in v1:
time: 941 us
  waiting for transfers between devices  711 us (76%)
  blocking collectives  187 us (20%)
  between operations  14.8 us (2%)
  local copies, waits for them, and re-layouts  13.6 us (1%)
  matrix products  10.8 us (1%)
    unnamed x2, waiting for transfers between devices  711 us
    all_gather x1, blocking collectives, local(): sigma_diag = jnp.sum(lax.all_gather(partial_contribution, 'pair'), axis=0)  181 us
  transfers between devices with their start and end apart: 1, of which 1 were waited for; matrix products, arithmetic and copies ran while one was open for 0% of the time, Pallas kernels for 0%

profile of v1, /device:TPU:2, one launch (start us, length us, event | category | flops | bytes accessed | tf_op | source)
XLA Modules:
  0.0 940.7 jit_solution(4306599785058071764)
XLA Ops:
  7.2 0.0 all-reduce.3.cloned.1.call-start
  7.2 0.0 copy-start.1
  7.2 0.0 copy-start.3
  7.2 1.6 dynamic-slice_convert_fusion
  8.9 2.3 copy.16
  11.2 0.0 copy-done.1
  11.2 0.0 copy-done.3
  11.2 0.3 select_reduce_fusion
  11.5 9.9 %negate_bitcast_fusion = f32[1536,2,384]{0,2,1:T(8,128)} fusion(bf16[2048,1536]{1,0:T(8,128)(2,1)} %param.5, f32[2048,384]{0,1:T(8,128)} %copy.16, f32[2,2048]{1,0:T(2,128)S(1)} %multiply_bitcast_fusion), kind=kOutput, calls=%fused_computation.3 | convolution fusion | flops 4836163584 | bytes 14172160 | tf_op jit(solution)/shard_map/zh,vzo->hvo/dot_general | solution.py:30
  21.4 8.2 copy.17
  29.6 0.0 copy-start.2
  29.6 0.0 copy-start.4
  29.6 0.0 copy-start
  29.6 0.0 all-reduce.3.cloned.1.call-update
  29.6 0.7 copy-done.2
  30.3 0.1 dynamic_slice.14
  30.4 0.1 dynamic_slice.12
  30.4 0.0 copy-done.4
  30.4 0.6 dynamic-slice
  31.7 0.0 copy-done
  31.7 711.5 %all-reduce.3.cloned.1.call-done = f32[1536,2,384]{2,1,0:T(2,128)} async-done(((f32[1536,2,384]{2,1,0:T(2,128)}), f32[1536,2,384]{2,1,0:T(2,128)}) %all-reduce.3.cloned.1.call-update) | async-done | bytes 4718608
  743.2 0.9 constant_dynamic-slice_fusion
  744.1 0.1 fusion.8
  744.2 5.9 all_gather.7
  750.0 0.9 multiply_reduce_fusion
  751.0 181.4 %all-gather.1 = f32[64,2,512]{2,1,0:T(2,128)S(1)} all-gather(f32[1,2,512]{2,1,0:T(2,128)S(1)} %multiply_bitcast_fusion.1), channel_id=2, replica_groups=mesh['pair'=64,'sigma'=4] {'pair'}, dimensions={0}, use_global_device_ids=true | all-gather | bytes 266240 | tf_op jit(solution)/shard_map/all_gather | solution.py:52
  932.4 0.7 copy.19
  933.1 0.7 reduce_sum.29
  (4 shorter events, 0.0 us)
Async XLA Ops:
  7.2 736.0 %all-reduce.3.cloned.1.call-start = ((), (), s32[]{:S(2)}) async-start(), calls=%async_computation | async-start | bytes 9437184
  7.2 4.0 copy-start.1
  7.2 4.0 copy-start.3
  29.6 0.7 copy-start.2
  29.6 0.9 copy-start.4
  29.6 2.1 copy-start
Sparse Core Ops, SparseCore 0:
  29.7 713.4 all-reduce.2
